TPU v7x, 32 devices: a whole 2x2x4 slice. The times are simulated.
32 devices in a mesh: dp: 8 (over z, y), tensor: 4 (over x, core).
Axes of the slice: x: 2, y: 2, z: 4, core: 2. Of those that a mesh axis runs over, the one named last changes fastest.
Arguments:
- tokens: bfloat16 [8192, 1024], P('dp', 'tensor'), may hold values from -6 to 6
- dealing: int32 [8192], P('dp'), may hold values from 0 to 8191, as said below
- seq_ids: int32 [8192], P('dp'), may hold values from 0 to 8191, as said below
- first_values: bfloat16 [8192, 1024], P('dp', 'tensor'), may hold values from -6 to 6
- out_grad: bfloat16 [8192, 1024], P('dp', 'tensor'), may hold values from -6 to 6
- norm1_gain: bfloat16 [1024], replicated, may hold values from 0.5 to 1.5
- norm2_gain: bfloat16 [1024], replicated, may hold values from 0.5 to 1.5
- w_query: bfloat16 [1024, 1024], P(None, 'tensor'), may hold values from -0.1875 to 0.1875
- w_key: bfloat16 [1024, 1024], P(None, 'tensor'), may hold values from -0.1875 to 0.1875
- w_value: bfloat16 [1024, 1024], P(None, 'tensor'), may hold values from -0.1875 to 0.1875
- w_out: bfloat16 [1024, 1024], P('tensor'), may hold values from -1 to 1
- w_gate: bfloat16 [1024, 2816], P(None, 'tensor'), may hold values from -0.1875 to 0.1875
- w_up: bfloat16 [1024, 2816], P(None, 'tensor'), may hold values from -0.1875 to 0.1875
- w_down: bfloat16 [2816, 1024], P('tensor'), may hold values from -0.109375 to 0.109375
Outputs:
- output: bfloat16 [8192, 1024], P('dp', 'tensor')
- input_grad: bfloat16 [8192, 1024], P('dp', 'tensor')
- first_values_grad: bfloat16 [8192, 1024], P('dp', 'tensor')
- norm1_gain_grad: float32 [4, 256], P('tensor', 'dp')
- norm2_gain_grad: float32 [4, 256], P('tensor', 'dp')
- w_query_grad: float32 [1024, 1024], P('dp', 'tensor')
- w_key_grad: float32 [1024, 1024], P('dp', 'tensor')
- w_value_grad: float32 [1024, 1024], P('dp', 'tensor')
- w_out_grad: float32 [1024, 1024], P('tensor', 'dp')
- w_gate_grad: float32 [1024, 2816], P('dp', 'tensor')
- w_up_grad: float32 [1024, 2816], P('dp', 'tensor')
- w_down_grad: float32 [2816, 1024], P('tensor', 'dp')
Inputs may be any that keep to these rules, and one draw needn't show every extreme that they name: `dealing`: a permutation; the tokens of each dp index go evenly, 1024 / 8 of them, to the rows of each dp index's block of 1024 dealt rows. `seq_ids`: never fall; no sequence crosses a multiple of 1024 rows; in every draw some block of 1024 rows is a single sequence; the rows of block b carry ids from b * 1024 to b * 1024 + 1023.
All inputs are finite; a program needn't handle non-finite values.
Results may differ from a plain program's by a relative error of at most 0.013.
Values may be sent and summed in bfloat16 or wider, within the bound.
No kernel may reach another device: no remote copies, remote signals or barrier semaphores. Data moves between devices by JAX's collectives and lax.ppermute only.
A program may use at most 128 MiB of HBM per device.

v0:
```python
import jax
import jax.numpy as jnp
from jax import lax
from jax.sharding import PartitionSpec as P

HEAD_DIM = 64
EPS = 1e-06
THETA = 10000.0
NEG = -1e30


def rope_tables(seq_row, head_dim):
    count = seq_row.shape[0]
    places = jnp.arange(count, dtype=jnp.int32)
    change = jnp.concatenate([jnp.ones((1,), bool), seq_row[1:] != seq_row[:-1]])
    starts = lax.cummax(jnp.where(change, places, jnp.zeros_like(places)), axis=0)
    offset = (places - starts).astype(jnp.float32)
    half = head_dim // 2
    freqs = THETA ** (-jnp.arange(half, dtype=jnp.float32) / half)
    angles = offset[:, None] * freqs[None, :]
    return (jnp.cos(angles), jnp.sin(angles))


def rotate(values, cos_rows, sin_rows):
    count = values.shape[0]
    half = cos_rows.shape[1]
    parts = values.reshape(count, -1, 2, half)
    first = parts[:, :, 0]
    second = parts[:, :, 1]
    cos_b = cos_rows[:, None, :]
    sin_b = sin_rows[:, None, :]
    return jnp.stack(
        [first * cos_b - second * sin_b, second * cos_b + first * sin_b], axis=2
    ).reshape(count, -1)


def rotate_back(grads, cos_rows, sin_rows):
    count = grads.shape[0]
    half = cos_rows.shape[1]
    parts = grads.reshape(count, -1, 2, half)
    first = parts[:, :, 0]
    second = parts[:, :, 1]
    cos_b = cos_rows[:, None, :]
    sin_b = sin_rows[:, None, :]
    return jnp.stack(
        [first * cos_b + second * sin_b, second * cos_b - first * sin_b], axis=2
    ).reshape(count, -1)


def row_total(values):
    return lax.psum(values, "tensor")


def gather_normed(normed):
    return lax.all_gather(normed, "tensor", axis=1, tiled=True)


def branch_sum(term):
    return lax.psum_scatter(term, "tensor", scatter_dimension=1, tiled=True)


def gather_grad(grads):
    return lax.all_gather(grads, "tensor", axis=1, tiled=True)


def input_sum(term):
    return lax.psum_scatter(term, "tensor", scatter_dimension=1, tiled=True)


def norm_forward(resid, gain):
    width = resid.shape[1] * lax.axis_size("tensor")
    total = row_total(jnp.sum(resid * resid, axis=1))
    scale = lax.rsqrt(total / width + EPS)[:, None]
    normed = (resid * scale * gain).astype(jnp.bfloat16)
    return (gather_normed(normed), scale)


def norm_backward(dnormed, resid, scale, gain):
    width = resid.shape[1] * lax.axis_size("tensor")
    weighted = dnormed * gain
    dot_row = row_total(jnp.sum(weighted * resid, axis=1))[:, None]
    dresid = scale * weighted - resid * (scale * scale * scale) * dot_row / width
    dgain = jnp.sum(dnormed * resid * scale, axis=0)
    return (dresid, dgain)


def block_mask(seq_block, seq_row, start):
    block = seq_block.shape[0]
    count = seq_row.shape[0]
    rows = start + jnp.arange(block, dtype=jnp.int32)
    cols = jnp.arange(count, dtype=jnp.int32)
    return (seq_block[:, None] == seq_row[None, :]) & (cols[None, :] <= rows[:, None])


def attend(queries, keys, values, seq_row, block):
    count, heads, depth = queries.shape
    blocks = count // block
    factor = depth ** (-0.5)
    query_blocks = queries.reshape(blocks, block, heads, depth)
    seq_blocks = seq_row.reshape(blocks, block)
    starts = jnp.arange(blocks, dtype=jnp.int32) * block

    def one_block(items):
        query_block, seq_block, start = items
        scores = (
            jnp.einsum("qhd,khd->hqk", query_block, keys, preferred_element_type=jnp.float32)
            * factor
        )
        mask = block_mask(seq_block, seq_row, start)
        scores = jnp.where(mask[None], scores, NEG)
        top = jnp.max(scores, axis=-1, keepdims=True)
        expo = jnp.exp(scores - top)
        total = jnp.sum(expo, axis=-1, keepdims=True)
        probs = expo / total
        result = jnp.einsum(
            "hqk,khd->qhd", probs.astype(jnp.bfloat16), values, preferred_element_type=jnp.float32
        )
        return (result.astype(jnp.bfloat16), (top + jnp.log(total))[:, :, 0])

    results, log_totals = lax.map(one_block, (query_blocks, seq_blocks, starts))
    return (results.reshape(count, heads * depth), log_totals)


def attend_back(queries, keys, values, seq_row, log_totals, dattn, block):
    count, heads, depth = queries.shape
    blocks = count // block
    factor = depth ** (-0.5)
    query_blocks = queries.reshape(blocks, block, heads, depth)
    seq_blocks = seq_row.reshape(blocks, block)
    grad_blocks = dattn.reshape(blocks, block, heads, depth)
    starts = jnp.arange(blocks, dtype=jnp.int32) * block

    def one_back(carry, items):
        dkey_acc, dval_acc = carry
        query_block, seq_block, start, log_block, grad_block = items
        scores = (
            jnp.einsum("qhd,khd->hqk", query_block, keys, preferred_element_type=jnp.float32)
            * factor
        )
        mask = block_mask(seq_block, seq_row, start)
        probs = jnp.where(mask[None], jnp.exp(scores - log_block[:, :, None]), 0.0)
        dval_acc = dval_acc + jnp.einsum(
            "hqk,qhd->khd",
            probs.astype(jnp.bfloat16),
            grad_block,
            preferred_element_type=jnp.float32,
        )
        dprob = jnp.einsum("qhd,khd->hqk", grad_block, values, preferred_element_type=jnp.float32)
        delta = jnp.sum(probs * dprob, axis=-1, keepdims=True)
        dscore = (probs * (dprob - delta)).astype(jnp.bfloat16)
        dquery = (
            jnp.einsum("hqk,khd->qhd", dscore, keys, preferred_element_type=jnp.float32) * factor
        )
        dkey_acc = (
            dkey_acc
            + jnp.einsum("hqk,qhd->khd", dscore, query_block, preferred_element_type=jnp.float32)
            * factor
        )
        return ((dkey_acc, dval_acc), dquery)

    zeros = jnp.zeros((count, heads, depth), jnp.float32)
    (dkeys, dvals), dqueries = lax.scan(
        one_back, (zeros, zeros), (query_blocks, seq_blocks, starts, log_totals, grad_blocks)
    )
    return (
        dqueries.reshape(count, heads * depth),
        dkeys.reshape(count, heads * depth),
        dvals.reshape(count, heads * depth),
    )


def per_device(
    tokens,
    dealing,
    seq_ids,
    first_values,
    out_grad,
    norm1_gain,
    norm2_gain,
    w_query,
    w_key,
    w_value,
    w_out,
    w_gate,
    w_up,
    w_down,
):
    order = jnp.argsort(dealing)
    arrived = (
        lax.all_to_all(tokens[order], "dp", split_axis=0, concat_axis=0, tiled=True),
        lax.all_to_all(first_values[order], "dp", split_axis=0, concat_axis=0, tiled=True),
        lax.all_to_all(out_grad[order], "dp", split_axis=0, concat_axis=0, tiled=True),
        lax.all_to_all(dealing[order], "dp", split_axis=0, concat_axis=0, tiled=True),
    )
    in_rows, in_first, in_grad, in_slots = arrived
    count = in_rows.shape[0]
    local_slot = in_slots % count
    arrange = jnp.argsort(local_slot)
    resid = in_rows[arrange].astype(jnp.float32)
    first_rows = in_first[arrange].astype(jnp.float32)
    grad_bf = in_grad[arrange]
    shard = resid.shape[1]
    rank = lax.axis_index("tensor")
    gain1 = lax.dynamic_slice_in_dim(norm1_gain, rank * shard, shard).astype(jnp.float32)
    gain2 = lax.dynamic_slice_in_dim(norm2_gain, rank * shard, shard).astype(jnp.float32)
    cos_rows, sin_rows = rope_tables(seq_ids, HEAD_DIM)
    heads = w_query.shape[1] // HEAD_DIM
    block = min(512, count)
    normed1, scale1 = norm_forward(resid, gain1)
    query_pre = jnp.dot(normed1, w_query, preferred_element_type=jnp.float32)
    key_pre = jnp.dot(normed1, w_key, preferred_element_type=jnp.float32)
    value_pre = jnp.dot(normed1, w_value, preferred_element_type=jnp.float32)
    queries = (
        rotate(query_pre, cos_rows, sin_rows).astype(jnp.bfloat16).reshape(count, heads, HEAD_DIM)
    )
    keys = rotate(key_pre, cos_rows, sin_rows).astype(jnp.bfloat16).reshape(count, heads, HEAD_DIM)
    values = (
        (0.5 * value_pre + 0.5 * first_rows).astype(jnp.bfloat16).reshape(count, heads, HEAD_DIM)
    )
    attended, log_totals = attend(queries, keys, values, seq_ids, block)
    middle = resid + branch_sum(jnp.dot(attended, w_out, preferred_element_type=jnp.float32))
    normed2, scale2 = norm_forward(middle, gain2)
    gate = jnp.dot(normed2, w_gate, preferred_element_type=jnp.float32)
    upval = jnp.dot(normed2, w_up, preferred_element_type=jnp.float32)
    sigmoid = jax.nn.sigmoid(gate)
    hidden = (gate * sigmoid * upval).astype(jnp.bfloat16)
    result = (
        middle + branch_sum(jnp.dot(hidden, w_down, preferred_element_type=jnp.float32))
    ).astype(jnp.bfloat16)
    full_grad = gather_grad(grad_bf)
    grad_down = jnp.einsum("tf,td->fd", hidden, full_grad, preferred_element_type=jnp.float32)
    grad_hidden = jnp.einsum("td,fd->tf", full_grad, w_down, preferred_element_type=jnp.float32)
    grad_up = (grad_hidden * gate * sigmoid).astype(jnp.bfloat16)
    grad_gate = (grad_hidden * upval * sigmoid * (1.0 + gate * (1.0 - sigmoid))).astype(
        jnp.bfloat16
    )
    grad_wgate = jnp.einsum("td,tf->df", normed2, grad_gate, preferred_element_type=jnp.float32)
    grad_wup = jnp.einsum("td,tf->df", normed2, grad_up, preferred_element_type=jnp.float32)
    dnormed2 = input_sum(
        jnp.einsum("tf,df->td", grad_gate, w_gate, preferred_element_type=jnp.float32)
        + jnp.einsum("tf,df->td", grad_up, w_up, preferred_element_type=jnp.float32)
    )
    dmiddle_norm, dgain2 = norm_backward(dnormed2, middle, scale2, gain2)
    dmiddle = grad_bf.astype(jnp.float32) + dmiddle_norm
    full_attn_grad = gather_grad(dmiddle.astype(jnp.bfloat16))
    grad_wout = jnp.einsum(
        "tc,td->cd", attended, full_attn_grad, preferred_element_type=jnp.float32
    )
    dattn = jnp.einsum(
        "td,cd->tc", full_attn_grad, w_out, preferred_element_type=jnp.float32
    ).astype(jnp.bfloat16)
    dqueries, dkeys, dvals = attend_back(queries, keys, values, seq_ids, log_totals, dattn, block)
    dquery_pre = rotate_back(dqueries, cos_rows, sin_rows).astype(jnp.bfloat16)
    dkey_pre = rotate_back(dkeys, cos_rows, sin_rows).astype(jnp.bfloat16)
    half_dval = (0.5 * dvals.astype(jnp.bfloat16).astype(jnp.float32)).astype(jnp.bfloat16)
    grad_wquery = jnp.einsum("td,tc->dc", normed1, dquery_pre, preferred_element_type=jnp.float32)
    grad_wkey = jnp.einsum("td,tc->dc", normed1, dkey_pre, preferred_element_type=jnp.float32)
    grad_wvalue = jnp.einsum("td,tc->dc", normed1, half_dval, preferred_element_type=jnp.float32)
    dnormed1 = input_sum(
        jnp.einsum("tc,dc->td", dquery_pre, w_query, preferred_element_type=jnp.float32)
        + jnp.einsum("tc,dc->td", dkey_pre, w_key, preferred_element_type=jnp.float32)
        + jnp.einsum("tc,dc->td", half_dval, w_value, preferred_element_type=jnp.float32)
    )
    dresid_norm, dgain1 = norm_backward(dnormed1, resid, scale1, gain1)
    dresid = (dmiddle + dresid_norm).astype(jnp.bfloat16)
    summed = (
        lax.psum_scatter(grad_wquery, "dp", scatter_dimension=0, tiled=True),
        lax.psum_scatter(grad_wkey, "dp", scatter_dimension=0, tiled=True),
        lax.psum_scatter(grad_wvalue, "dp", scatter_dimension=0, tiled=True),
        lax.psum_scatter(grad_wout, "dp", scatter_dimension=1, tiled=True),
        lax.psum_scatter(grad_wgate, "dp", scatter_dimension=0, tiled=True),
        lax.psum_scatter(grad_wup, "dp", scatter_dimension=0, tiled=True),
        lax.psum_scatter(grad_down, "dp", scatter_dimension=1, tiled=True),
        lax.psum_scatter(dgain1[None, :], "dp", scatter_dimension=1, tiled=True),
        lax.psum_scatter(dgain2[None, :], "dp", scatter_dimension=1, tiled=True),
    )
    returned = (
        lax.all_to_all(result[local_slot], "dp", split_axis=0, concat_axis=0, tiled=True),
        lax.all_to_all(dresid[local_slot], "dp", split_axis=0, concat_axis=0, tiled=True),
        lax.all_to_all(half_dval[local_slot], "dp", split_axis=0, concat_axis=0, tiled=True),
    )
    restore = jnp.argsort(order)
    output = returned[0][restore]
    input_grad = returned[1][restore]
    first_grad = returned[2][restore]
    return (
        output,
        input_grad,
        first_grad,
        summed[7],
        summed[8],
        summed[0],
        summed[1],
        summed[2],
        summed[3],
        summed[4],
        summed[5],
        summed[6],
    )


def solution(mesh):
    in_specs = (
        P("dp", "tensor"),
        P("dp"),
        P("dp"),
        P("dp", "tensor"),
        P("dp", "tensor"),
        P(),
        P(),
        P(None, "tensor"),
        P(None, "tensor"),
        P(None, "tensor"),
        P("tensor", None),
        P(None, "tensor"),
        P(None, "tensor"),
        P("tensor", None),
    )
    out_specs = (
        P("dp", "tensor"),
        P("dp", "tensor"),
        P("dp", "tensor"),
        P("tensor", "dp"),
        P("tensor", "dp"),
        P("dp", "tensor"),
        P("dp", "tensor"),
        P("dp", "tensor"),
        P("tensor", "dp"),
        P("dp", "tensor"),
        P("dp", "tensor"),
        P("tensor", "dp"),
    )
    return jax.shard_map(
        per_device, mesh=mesh, in_specs=in_specs, out_specs=out_specs, check_vma=False
    )
```

profile of v0, /device:TPU:0, one launch (start us, length us, event | category | flops | bytes accessed | tf_op | source)
XLA Modules:
  0.0 1110.9 jit_solution(10349196735572572018)
XLA Ops:
  12.4 8.8 gather_fusion.1
  21.3 7.3 all-to-all-start.1
  44.8 8.8 all-to-all-done
  77.3 10.9 all-to-all-done.2
  100.1 20.7 %while.27 = (s32[]{:T(128)}, bf16[2,512,4,64]{1,3,2,0:T(8,128)(2,1)}, f32[2,4,512]{2,1,0:T(4,128)}, s32[2,512]{1,0:T(2,128)S(1)}, s32[1024]{0:T(1024)S(1)}, /*in...) while((s32[]{:T(128)}, ...), condition=%wide.region_9.10_spmd, body=%wide.region_6.9_spmd.sunk | while | flops 563739136 | bytes 33241340 | solution.py:120
  128.7 42.2 %reduce-scatter.18.cloned.1.call-done = f32[1024,256]{1,0:T(8,128)} async-done(((f32[1024,1024]{1,0:T(8,128)}), f32[1024,256]{1,0:T(8,128)}) %reduce-scatter.18.cloned.1.call-update) | async-done | bytes 1048592 | tf_op jit(solution)/shard_map/reduce_scatter | solution.py:59
  186.9 20.0 %all_to_all.87 = bf16[8,128,256]{2,1,0:T(8,128)(2,1)S(1)} all-to-all(bf16[8,128,256]{2,1,0:T(8,128)(2,1)} %bitcast.210), channel_id=1, replica_groups=mesh['dp'=8,'tensor'=4] {'dp'}, dimensions={0} | all-to-all | bytes 1048576 | tf_op jit(solution)/shard_map/all_to_all | solution.py:192
  221.1 12.1 %all-gather.12.cloned.1.call-done = bf16[1024,1024]{1,0:T(8,128)(2,1)} async-done(((bf16[1024,256]{1,0:T(8,128)(2,1)}), bf16[1024,1024]{1,0:T(8,128)(2,1)}) %all-gather.12.cloned.1.call-update) | async-done | bytes 2097168 | tf_op jit(solution)/shard_map/all_gather | solution.py:63
  233.2 6.3 multiply_convert_fusion.1
  251.3 39.3 %reduce-scatter.22.cloned.1.call-done = f32[1024,256]{1,0:T(8,128)} async-done(((f32[1024,1024]{1,0:T(8,128)}), f32[1024,256]{1,0:T(8,128)}) %reduce-scatter.22.cloned.1.call-update) | async-done | bytes 1048592 | tf_op jit(solution)/shard_map/reduce_scatter | solution.py:67
  298.0 39.5 %reduce-scatter.20.cloned.1.call-done = f32[1024,256]{1,0:T(8,128)} async-done(((f32[1024,1024]{1,0:T(8,128)}), f32[1024,256]{1,0:T(8,128)}) %reduce-scatter.20.cloned.1.call-update) | async-done | bytes 1048592 | tf_op jit(solution)/shard_map/reduce_scatter | solution.py:59
  341.2 22.7 %all-gather.10.cloned.1.call-done = bf16[1024,1024]{1,0:T(8,128)(2,1)} async-done(((bf16[1024,256]{1,0:T(8,128)(2,1)}), bf16[1024,1024]{1,0:T(8,128)(2,1)}) %all-gather.10.cloned.1.call-update) | async-done | bytes 2097168 | tf_op jit(solution)/shard_map/all_gather | solution.py:63
  372.2 55.5 %while.28 = (s32[]{:T(128)}, f32[1024,4,64]{0,2,1:T(8,128)S(1)}, f32[1024,4,64]{0,2,1:T(8,128)}, f32[2,512,4,64]{1,0,3,2:T(2,128)}, bf16[2,512,4,64]{1,3,2,0:T(8...) while((s32[]{:T(128)}, f32[1024,4,64]{0,2,1:T(8,128)S(1)}, ...), condition=%wide.region_20.21_spmd.clone, body=%wide.region_18.20_spmd.clone.sunk | while | flops 1376647680 | bytes 74520776 | solution.py:162
  389.1 10.4 dynamic_update_slice.20
  416.9 10.4 dynamic_update_slice.20
  437.5 43.8 %reduce-scatter.24.cloned.1.call-done = f32[1024,256]{1,0:T(8,128)} async-done(((f32[1024,1024]{1,0:T(8,128)}), f32[1024,256]{1,0:T(8,128)}) %reduce-scatter.24.cloned.1.call-update) | async-done | bytes 1048592 | tf_op jit(solution)/shard_map/reduce_scatter | solution.py:67
  571.7 39.8 %reduce-scatter.40.cloned.1.call-done = f32[32,1]{1,0:T(8,128)} async-done(((f32[256,1]{1,0:T(8,128)}), f32[32,1]{1,0:T(8,128)}) %reduce-scatter.40.cloned.1.call-update) | async-done | bytes 144
  617.8 69.2 %reduce-scatter.38.cloned.1.call-done = f32[704,128]{1,0:T(8,128)} async-done(((f32[704,1024]{1,0:T(8,128)}), f32[704,128]{1,0:T(8,128)}) %reduce-scatter.38.cloned.1.call-update) | async-done | bytes 360464 | tf_op jit(solution)/shard_map/reduce_scatter | solution.py:273
  686.9 75.3 %reduce-scatter.36.cloned.1.call-done = f32[128,704]{0,1:T(8,128)} async-done(((f32[1024,704]{0,1:T(8,128)}), f32[128,704]{0,1:T(8,128)}) %reduce-scatter.36.cloned.1.call-update) | async-done | bytes 360464 | tf_op jit(solution)/shard_map/reduce_scatter | solution.py:272
  762.3 75.5 %reduce-scatter.34.cloned.1.call-done = f32[128,704]{0,1:T(8,128)} async-done(((f32[1024,704]{0,1:T(8,128)}), f32[128,704]{0,1:T(8,128)}) %reduce-scatter.34.cloned.1.call-update) | async-done | bytes 360464 | tf_op jit(solution)/shard_map/reduce_scatter | solution.py:271
  837.7 66.9 %reduce-scatter.32.cloned.1.call-done = f32[256,128]{1,0:T(8,128)} async-done(((f32[256,1024]{1,0:T(8,128)}), f32[256,128]{1,0:T(8,128)}) %reduce-scatter.32.cloned.1.call-update) | async-done | bytes 131088 | tf_op jit(solution)/shard_map/reduce_scatter | solution.py:270
  904.6 66.6 %reduce-scatter.30.cloned.1.call-done = f32[128,256]{1,0:T(8,128)} async-done(((f32[1024,256]{1,0:T(8,128)}), f32[128,256]{1,0:T(8,128)}) %reduce-scatter.30.cloned.1.call-update) | async-done | bytes 131088 | tf_op jit(solution)/shard_map/reduce_scatter | solution.py:269
  971.2 66.3 %reduce-scatter.28.cloned.1.call-done = f32[128,256]{1,0:T(8,128)} async-done(((f32[1024,256]{1,0:T(8,128)}), f32[128,256]{1,0:T(8,128)}) %reduce-scatter.28.cloned.1.call-update) | async-done | bytes 131088 | tf_op jit(solution)/shard_map/reduce_scatter | solution.py:268
  1037.5 66.7 %reduce-scatter.26.cloned.1.call-done = f32[128,256]{1,0:T(8,128)} async-done(((f32[1024,256]{1,0:T(8,128)}), f32[128,256]{1,0:T(8,128)}) %reduce-scatter.26.cloned.1.call-update) | async-done | bytes 131088 | tf_op jit(solution)/shard_map/reduce_scatter | solution.py:267
  (311 shorter events, 286.5 us)
Async XLA Ops:
  21.3 13.7 %all-to-all-start.1 = ((s32[8,128,1]{1,2,0:T(1,128)}), s32[8,128,1]{1,2,0:T(1,128)S(1)}, u32[]{:S(2)}, u32[]{:S(2)}) async-start(s32[8,128,1]{1,2,0:T(1,128)} %bitcast.9), calls=%async_computation.1 | async-start | bytes 8192 | tf_op jit(solution)/shard_map/all_to_all | solution.py:193
  34.9 18.6 %all-to-all-start = ((bf16[8,128,256]{2,1,0:T(8,128)(2,1)}), bf16[8,128,256]{2,1,0:T(8,128)(2,1)S(1)}, u32[]{:S(2)}, u32[]{:S(2)}) async-start(bf16[8,128,256]{2,1,0:T(8,128)(2,1)} %bitcast.6), calls=%async_computation | async-start | bytes 1048576 | tf_op jit(solution)/shard_map/all_to_all | solution.py:190
  39.5 53.7 %all-gather.6.cloned.1.call-start = ((), (), s32[]{:S(2)}) async-start(), calls=%async_computation.20 | async-start | bytes 2621440 | tf_op jit(solution)/shard_map/all_gather | solution.py:55
  70.0 18.3 %all-to-all-start.2 = ((bf16[8,128,256]{2,1,0:T(8,128)(2,1)}), bf16[8,128,256]{2,1,0:T(8,128)(2,1)S(1)}, u32[]{:S(2)}, u32[]{:S(2)}) async-start(bf16[8,128,256]{2,1,0:T(8,128)(2,1)} %bitcast.16), calls=%async_computation.2 | async-start | bytes 1048576 | tf_op jit(solution)/shard_map/all_to_all | solution.py:191
  74.3 96.6 %reduce-scatter.18.cloned.1.call-start = ((), (), s32[]{:S(2)}) async-start(), calls=%async_computation.21 | async-start | bytes 5242880 | tf_op jit(solution)/shard_map/reduce_scatter | solution.py:59
  127.3 85.1 %all-gather.8.cloned.1.call-start = ((), (), s32[]{:S(2)}) async-start(), calls=%async_computation.22 | async-start | bytes 2621440 | tf_op jit(solution)/shard_map/all_gather | solution.py:55
  181.8 51.4 %all-gather.12.cloned.1.call-start = ((), (), s32[]{:S(2)}) async-start(), calls=%async_computation.34 | async-start | bytes 2621440 | tf_op jit(solution)/shard_map/all_gather | solution.py:63
  212.1 78.5 %reduce-scatter.22.cloned.1.call-start = ((), (), s32[]{:S(2)}) async-start(), calls=%async_computation.24 | async-start | bytes 5242880 | tf_op jit(solution)/shard_map/reduce_scatter | solution.py:67
  245.9 91.6 %reduce-scatter.20.cloned.1.call-start = ((), (), s32[]{:S(2)}) async-start(), calls=%async_computation.23 | async-start | bytes 5242880 | tf_op jit(solution)/shard_map/reduce_scatter | solution.py:59
  251.2 112.7 %all-gather.10.cloned.1.call-start = ((), (), s32[]{:S(2)}) async-start(), calls=%async_computation.25 | async-start | bytes 2621440 | tf_op jit(solution)/shard_map/all_gather | solution.py:63
  340.9 140.3 %reduce-scatter.24.cloned.1.call-start = ((), (), s32[]{:S(2)}) async-start(), calls=%async_computation.26 | async-start | bytes 5242880 | tf_op jit(solution)/shard_map/reduce_scatter | solution.py:67
  436.6 123.8 %reduce-scatter.42.cloned.1.call-start = ((), (), s32[]{:S(2)}) async-start(), calls=%async_computation.36 | async-start | bytes 147456
  437.5 174.0 %reduce-scatter.40.cloned.1.call-start = ((), (), s32[]{:S(2)}) async-start(), calls=%async_computation.35 | async-start | bytes 147456
  483.9 203.1 %reduce-scatter.38.cloned.1.call-start = ((), (), s32[]{:S(2)}) async-start(), calls=%async_computation.33 | async-start | bytes 3244032 | tf_op jit(solution)/shard_map/reduce_scatter | solution.py:273
  488.5 273.7 %reduce-scatter.36.cloned.1.call-start = ((), (), s32[]{:S(2)}) async-start(), calls=%async_computation.32 | async-start | bytes 3244032 | tf_op jit(solution)/shard_map/reduce_scatter | solution.py:272
  494.8 342.9 %reduce-scatter.34.cloned.1.call-start = ((), (), s32[]{:S(2)}) async-start(), calls=%async_computation.31 | async-start | bytes 3244032 | tf_op jit(solution)/shard_map/reduce_scatter | solution.py:271
  499.5 405.1 %reduce-scatter.32.cloned.1.call-start = ((), (), s32[]{:S(2)}) async-start(), calls=%async_computation.30 | async-start | bytes 1179648 | tf_op jit(solution)/shard_map/reduce_scatter | solution.py:270
  503.8 467.4 %reduce-scatter.30.cloned.1.call-start = ((), (), s32[]{:S(2)}) async-start(), calls=%async_computation.29 | async-start | bytes 1179648 | tf_op jit(solution)/shard_map/reduce_scatter | solution.py:269
  505.7 531.8 %reduce-scatter.28.cloned.1.call-start = ((), (), s32[]{:S(2)}) async-start(), calls=%async_computation.28 | async-start | bytes 1179648 | tf_op jit(solution)/shard_map/reduce_scatter | solution.py:268
  513.7 20.0 %all-to-all-start.3 = ((bf16[8,128,256]{2,1,0:T(8,128)(2,1)}), bf16[8,128,256]{2,1,0:T(8,128)(2,1)S(1)}, u32[]{:S(2)}, u32[]{:S(2)}) async-start(bf16[8,128,256]{2,1,0:T(8,128)(2,1)} %bitcast.209), calls=%async_computation.5 | async-start | bytes 1048576 | tf_op jit(solution)/shard_map/all_to_all | solution.py:278
  519.2 584.9 %reduce-scatter.26.cloned.1.call-start = ((), (), s32[]{:S(2)}) async-start(), calls=%async_computation.27 | async-start | bytes 1179648 | tf_op jit(solution)/shard_map/reduce_scatter | solution.py:267
  533.7 18.6 %all-to-all-start.6 = ((bf16[8,128,256]{2,1,0:T(8,128)(2,1)}), bf16[8,128,256]{2,1,0:T(8,128)(2,1)S(1)}, u32[]{:S(2)}, u32[]{:S(2)}) async-start(bf16[8,128,256]{2,1,0:T(8,128)(2,1)} %bitcast.31), calls=%async_computation.10 | async-start | bytes 1048576 | tf_op jit(solution)/shard_map/all_to_all | solution.py:280
  552.3 60.5 %all-to-all-start.5 = ((bf16[8,128,256]{2,1,0:T(8,128)(2,1)}), bf16[8,128,256]{2,1,0:T(8,128)(2,1)S(1)}, u32[]{:S(2)}, u32[]{:S(2)}) async-start(bf16[8,128,256]{2,1,0:T(8,128)(2,1)} %bitcast.29), calls=%async_computation.9 | async-start | bytes 1048576 | tf_op jit(solution)/shard_map/all_to_all | solution.py:279
  566.7 537.5 %copy-start.1 = (bf16[704,1024]{1,0:T(8,128)(2,1)S(1)}, bf16[704,1024]{1,0:T(8,128)(2,1)}, u32[]{:S(2)}) copy-start(bf16[704,1024]{1,0:T(8,128)(2,1)} %param.31) | copy-start | bytes 4325380
  (64 other events, 1202.8 us)
Sparse Core Ops, SparseCore 0:
  65.1 22.1 all-gather.5
  127.4 43.4 reduce-scatter.17
  181.9 23.9 all-gather.7
  212.2 20.9 all-gather.11
  246.0 44.5 reduce-scatter.21
  293.0 44.4 reduce-scatter.19
  341.1 22.8 all-gather.9
  436.7 44.5 reduce-scatter.23
  484.6 62.1 reduce-scatter.41
  549.9 61.5 reduce-scatter.39
  615.6 71.2 reduce-scatter.37
  690.9 71.3 reduce-scatter.35
  766.4 71.2 reduce-scatter.33
  841.5 62.9 reduce-scatter.31
  908.8 62.3 reduce-scatter.29
  975.1 62.3 reduce-scatter.27
  1041.7 62.4 reduce-scatter.25
where the time goes:
time: 1120 us; the launch traced here: 1110 us
  waiting for transfers between devices  756 us (68%)
  local copies, waits for them, and re-layouts  114 us (10%)
  matrix products  102 us (9%)
  other arithmetic  50.5 us (5%)
  blocking collectives  43.2 us (4%)
  starting transfers between devices  30.6 us (3%)
  between operations  14.9 us (1%)
    reduce_scatter x2, waiting for transfers between devices, input_sum(): return lax.psum_scatter(term, 'tensor', scatter_dimension=1, tiled=True)  83.1 us
    reduce_scatter x2, waiting for transfers between devices, branch_sum(): return lax.psum_scatter(term, 'tensor', scatter_dimension=1, tiled=True)  81.7 us
    reduce_scatter x1, waiting for transfers between devices, per_device(): lax.psum_scatter(grad_wgate, 'dp', scatter_dimension=0, tiled=True)  75.5 us
    reduce_scatter x1, waiting for transfers between devices, per_device(): lax.psum_scatter(grad_wup, 'dp', scatter_dimension=0, tiled=True)  75.3 us
    reduce_scatter x1, waiting for transfers between devices, per_device(): lax.psum_scatter(grad_down, 'dp', scatter_dimension=1, tiled=True)  69.2 us
    reduce_scatter x1, waiting for transfers between devices, per_device(): lax.psum_scatter(grad_wout, 'dp', scatter_dimension=1, tiled=True)  66.9 us
    reduce_scatter x1, waiting for transfers between devices, per_device(): lax.psum_scatter(grad_wquery, 'dp', scatter_dimension=0, tiled=True)  66.7 us
    reduce_scatter x1, waiting for transfers between devices, per_device(): lax.psum_scatter(grad_wvalue, 'dp', scatter_dimension=0, tiled=True)  66.6 us
  transfers between devices with their start and end apart: 23, of which 19 were waited for; matrix products, arithmetic and copies ran while one was open for 11% of the time, Pallas kernels for 0%

commit v1 on v0

--- a/solution.py
+++ b/solution.py
@@ -1,3 +1,4 @@
+import functools
 import jax
 import jax.numpy as jnp
 from jax import lax
@@ -7,6 +8,23 @@
 EPS = 1e-06
 THETA = 10000.0
 NEG = -1e30
+
+
+def _detail_layers_all(message, axis_name):
+    n_axis = lax.psum(1, axis_name=axis_name)
+    lanes = [(to_i, (to_i + 1) % n_axis) for to_i in range(n_axis)]
+    entries = [(to_i, (to_i - 1) % n_axis) for to_i in range(n_axis)]
+    vec_out, s_next = ([message], [message])
+    for _ in range(n_axis // 2):
+        vec_out.append(lax.ppermute(vec_out[-1], axis_name=axis_name, perm=lanes))
+    for _ in range((n_axis - 1) // 2):
+        s_next.append(lax.ppermute(s_next[-1], axis_name=axis_name, perm=entries))
+    r2 = jnp.concatenate([*vec_out[::-1], *s_next[1:]], axis=1)
+    e_now = jnp.roll(r2, shift=(lax.axis_index(axis_name) - n_axis // 2) * message.shape[1], axis=1)
+    return e_now
+
+
+detail_bars_for = functools.partial(_detail_layers_all, axis_name="tensor")
 
 
 def rope_tables(seq_row, head_dim):
@@ -60,7 +78,7 @@
 
 
 def gather_grad(grads):
-    return lax.all_gather(grads, "tensor", axis=1, tiled=True)
+    return detail_bars_for(grads)
 
 
 def input_sum(term):

time: 1120 us -> 1130 us (level)
    ppermute x0 -> x6, waiting for transfers between devices: none -> 41.2 us  [the longest x4 41.2 us: _detail_layers_all(): vec_out.append(lax.ppermute(vec_out[-1], axis_name=axis_name, perm=lanes))]
    all_gather x2 -> x0, waiting for transfers between devices: 34.8 us -> none  [gather_grad(): return lax.all_gather(grads, 'tensor', axis=1, tiled=True)]
    unnamed x19 -> x17, waiting for transfers between devices: 40.1 us -> 40.1 us
  transfers between devices with their start and end apart: 23 -> 27, of which waited for: 19 -> 21; matrix products, arithmetic and copies ran while one was open for 11% -> 10% of each run, Pallas kernels for 0% -> 0%
where the time goes in v1:
time: 1130 us; the launch traced here: 1120 us
  waiting for transfers between devices  760 us (67%)
  local copies, waits for them, and re-layouts  114 us (10%)
  matrix products  94.4 us (8%)
  other arithmetic  58.7 us (5%)
  blocking collectives  43.2 us (4%)
  starting transfers between devices  34 us (3%)
  between operations  15 us (1%)
    reduce_scatter x2, waiting for transfers between devices, branch_sum(): return lax.psum_scatter(term, 'tensor', scatter_dimension=1, tiled=True)  81.7 us
    reduce_scatter x2, waiting for transfers between devices, input_sum(): return lax.psum_scatter(term, 'tensor', scatter_dimension=1, tiled=True)  80.9 us
    reduce_scatter x1, waiting for transfers between devices, per_device(): lax.psum_scatter(grad_wgate, 'dp', scatter_dimension=0, tiled=True)  75.5 us
    reduce_scatter x1, waiting for transfers between devices, per_device(): lax.psum_scatter(grad_wup, 'dp', scatter_dimension=0, tiled=True)  75.3 us
    reduce_scatter x1, waiting for transfers between devices, per_device(): lax.psum_scatter(grad_down, 'dp', scatter_dimension=1, tiled=True)  69.2 us
    reduce_scatter x1, waiting for transfers between devices, per_device(): lax.psum_scatter(grad_wout, 'dp', scatter_dimension=1, tiled=True)  66.9 us
    reduce_scatter x1, waiting for transfers between devices, per_device(): lax.psum_scatter(grad_wvalue, 'dp', scatter_dimension=0, tiled=True)  66.9 us
    reduce_scatter x1, waiting for transfers between devices, per_device(): lax.psum_scatter(grad_wquery, 'dp', scatter_dimension=0, tiled=True)  66.7 us
  transfers between devices with their start and end apart: 27, of which 21 were waited for; matrix products, arithmetic and copies ran while one was open for 10% of the time, Pallas kernels for 0%

profile of v1, /device:TPU:0, one launch (start us, length us, event | category | flops | bytes accessed | tf_op | source)
XLA Modules:
  0.0 1120.3 jit_solution(9860333530502155369)
XLA Ops:
  12.4 8.8 gather_fusion.1
  44.8 8.8 all-to-all-done
  77.0 11.3 %all-to-all-done.2 = bf16[8,128,256]{2,1,0:T(8,128)(2,1)S(1)} async-done(((bf16[8,128,256]{2,1,0:T(8,128)(2,1)}), bf16[8,128,256]{2,1,0:T(8,128)(2,1)S(1)}, u32[]{:S(2)}, u32[]{:S(2)}) %all-to-all-start.2) | async-done | bytes 524320 | tf_op jit(solution)/shard_map/all_to_all | solution.py:209
  100.1 20.7 %while.27 = (s32[]{:T(128)}, bf16[2,512,4,64]{1,3,2,0:T(8,128)(2,1)}, f32[2,4,512]{2,1,0:T(4,128)}, s32[2,512]{1,0:T(2,128)S(1)}, s32[1024]{0:T(1024)S(1)}, /*in...) while((s32[]{:T(128)}, ...), condition=%wide.region_9.10_spmd, body=%wide.region_6.9_spmd.sunk | while | flops 563739136 | bytes 33241340 | solution.py:138
  128.6 42.2 %reduce-scatter.18.cloned.1.call-done = f32[1024,256]{1,0:T(8,128)} async-done(((f32[1024,1024]{1,0:T(8,128)}), f32[1024,256]{1,0:T(8,128)}) %reduce-scatter.18.cloned.1.call-update) | async-done | bytes 1048592 | tf_op jit(solution)/shard_map/reduce_scatter | solution.py:77
  186.9 19.9 %all_to_all.87 = bf16[8,128,256]{2,1,0:T(8,128)(2,1)S(1)} all-to-all(bf16[8,128,256]{2,1,0:T(8,128)(2,1)} %bitcast.210), channel_id=1, replica_groups=mesh['dp'=8,'tensor'=4] {'dp'}, dimensions={0} | all-to-all | bytes 1048576 | tf_op jit(solution)/shard_map/all_to_all | solution.py:210
  213.0 11.6 %collective-permute-done = bf16[1024,256]{1,0:T(8,128)(2,1)S(1)} collective-permute-done((bf16[1024,256]{1,0:T(8,128)(2,1)S(1)}, bf16[1024,256]{1,0:T(8,128)(2,1)S(1)}, u32[]{:S(2)}, u32[]{:S(2)}) %collective-permute-start) | collective-permute-done | bytes 524320 | tf_op jit(solution)/shard_map/ppermute | solution.py:19
  224.9 8.7 collective-permute-done.1
  259.4 37.4 %reduce-scatter.22.cloned.1.call-done = f32[1024,256]{1,0:T(8,128)} async-done(((f32[1024,1024]{1,0:T(8,128)}), f32[1024,256]{1,0:T(8,128)}) %reduce-scatter.22.cloned.1.call-update) | async-done | bytes 1048592 | tf_op jit(solution)/shard_map/reduce_scatter | solution.py:85
  304.2 39.5 %reduce-scatter.20.cloned.1.call-done = f32[1024,256]{1,0:T(8,128)} async-done(((f32[1024,1024]{1,0:T(8,128)}), f32[1024,256]{1,0:T(8,128)}) %reduce-scatter.20.cloned.1.call-update) | async-done | bytes 1048592 | tf_op jit(solution)/shard_map/reduce_scatter | solution.py:77
  348.6 12.0 %collective-permute-done.3 = bf16[1024,256]{1,0:T(8,128)(2,1)} collective-permute-done((bf16[1024,256]{1,0:T(8,128)(2,1)S(1)}, bf16[1024,256]{1,0:T(8,128)(2,1)}, u32[]{:S(2)}, u32[]{:S(2)}) %collective-permute-start.3) | collective-permute-done | bytes 524320 | tf_op jit(solution)/shard_map/ppermute | solution.py:19
  361.1 8.9 collective-permute-done.4
  381.7 55.2 %while.28 = (s32[]{:T(128)}, f32[1024,4,64]{0,2,1:T(8,128)S(1)}, f32[1024,4,64]{0,2,1:T(8,128)}, f32[2,512,4,64]{1,0,3,2:T(2,128)}, bf16[2,512,4,64]{1,3,2,0:T(8...) while((s32[]{:T(128)}, f32[1024,4,64]{0,2,1:T(8,128)S(1)}, ...), condition=%wide.region_20.22_spmd.clone, body=%wide.region_18.21_spmd.clone.sunk | while | flops 1376647680 | bytes 74520776 | solution.py:180
  398.7 10.4 dynamic_update_slice.20
  426.4 10.4 dynamic_update_slice.20
  446.8 43.5 %reduce-scatter.24.cloned.1.call-done = f32[1024,256]{1,0:T(8,128)} async-done(((f32[1024,1024]{1,0:T(8,128)}), f32[1024,256]{1,0:T(8,128)}) %reduce-scatter.24.cloned.1.call-update) | async-done | bytes 1048592 | tf_op jit(solution)/shard_map/reduce_scatter | solution.py:85
  580.6 39.9 %reduce-scatter.40.cloned.1.call-done = f32[32,1]{1,0:T(8,128)} async-done(((f32[256,1]{1,0:T(8,128)}), f32[32,1]{1,0:T(8,128)}) %reduce-scatter.40.cloned.1.call-update) | async-done | bytes 144
  626.8 69.2 %reduce-scatter.38.cloned.1.call-done = f32[704,128]{1,0:T(8,128)} async-done(((f32[704,1024]{1,0:T(8,128)}), f32[704,128]{1,0:T(8,128)}) %reduce-scatter.38.cloned.1.call-update) | async-done | bytes 360464 | tf_op jit(solution)/shard_map/reduce_scatter | solution.py:291
  696.0 75.3 %reduce-scatter.36.cloned.1.call-done = f32[128,704]{0,1:T(8,128)} async-done(((f32[1024,704]{0,1:T(8,128)}), f32[128,704]{0,1:T(8,128)}) %reduce-scatter.36.cloned.1.call-update) | async-done | bytes 360464 | tf_op jit(solution)/shard_map/reduce_scatter | solution.py:290
  771.3 75.5 %reduce-scatter.34.cloned.1.call-done = f32[128,704]{0,1:T(8,128)} async-done(((f32[1024,704]{0,1:T(8,128)}), f32[128,704]{0,1:T(8,128)}) %reduce-scatter.34.cloned.1.call-update) | async-done | bytes 360464 | tf_op jit(solution)/shard_map/reduce_scatter | solution.py:289
  846.8 66.9 %reduce-scatter.32.cloned.1.call-done = f32[256,128]{1,0:T(8,128)} async-done(((f32[256,1024]{1,0:T(8,128)}), f32[256,128]{1,0:T(8,128)}) %reduce-scatter.32.cloned.1.call-update) | async-done | bytes 131088 | tf_op jit(solution)/shard_map/reduce_scatter | solution.py:288
  913.7 66.9 %reduce-scatter.30.cloned.1.call-done = f32[128,256]{1,0:T(8,128)} async-done(((f32[1024,256]{1,0:T(8,128)}), f32[128,256]{1,0:T(8,128)}) %reduce-scatter.30.cloned.1.call-update) | async-done | bytes 131088 | tf_op jit(solution)/shard_map/reduce_scatter | solution.py:287
  980.5 66.3 %reduce-scatter.28.cloned.1.call-done = f32[128,256]{1,0:T(8,128)} async-done(((f32[1024,256]{1,0:T(8,128)}), f32[128,256]{1,0:T(8,128)}) %reduce-scatter.28.cloned.1.call-update) | async-done | bytes 131088 | tf_op jit(solution)/shard_map/reduce_scatter | solution.py:286
  1046.8 66.7 %reduce-scatter.26.cloned.1.call-done = f32[128,256]{1,0:T(8,128)} async-done(((f32[1024,256]{1,0:T(8,128)}), f32[128,256]{1,0:T(8,128)}) %reduce-scatter.26.cloned.1.call-update) | async-done | bytes 131088 | tf_op jit(solution)/shard_map/reduce_scatter | solution.py:285
  (319 shorter events, 304.9 us)
Async XLA Ops:
  21.3 13.7 %all-to-all-start.1 = ((s32[8,128,1]{1,2,0:T(1,128)}), s32[8,128,1]{1,2,0:T(1,128)S(1)}, u32[]{:S(2)}, u32[]{:S(2)}) async-start(s32[8,128,1]{1,2,0:T(1,128)} %bitcast.9), calls=%async_computation.1 | async-start | bytes 8192 | tf_op jit(solution)/shard_map/all_to_all | solution.py:211
  34.9 18.6 %all-to-all-start = ((bf16[8,128,256]{2,1,0:T(8,128)(2,1)}), bf16[8,128,256]{2,1,0:T(8,128)(2,1)S(1)}, u32[]{:S(2)}, u32[]{:S(2)}) async-start(bf16[8,128,256]{2,1,0:T(8,128)(2,1)} %bitcast.6), calls=%async_computation | async-start | bytes 1048576 | tf_op jit(solution)/shard_map/all_to_all | solution.py:208
  39.5 53.7 %all-gather.3.cloned.1.call-start = ((), (), s32[]{:S(2)}) async-start(), calls=%async_computation.20 | async-start | bytes 2621440 | tf_op jit(solution)/shard_map/all_gather | solution.py:73
  70.0 18.3 %all-to-all-start.2 = ((bf16[8,128,256]{2,1,0:T(8,128)(2,1)}), bf16[8,128,256]{2,1,0:T(8,128)(2,1)S(1)}, u32[]{:S(2)}, u32[]{:S(2)}) async-start(bf16[8,128,256]{2,1,0:T(8,128)(2,1)} %bitcast.16), calls=%async_computation.2 | async-start | bytes 1048576 | tf_op jit(solution)/shard_map/all_to_all | solution.py:209
  74.3 96.6 %reduce-scatter.18.cloned.1.call-start = ((), (), s32[]{:S(2)}) async-start(), calls=%async_computation.21 | async-start | bytes 5242880 | tf_op jit(solution)/shard_map/reduce_scatter | solution.py:77
  127.2 111.0 %all-gather.5.cloned.1.call-start = ((), (), s32[]{:S(2)}) async-start(), calls=%async_computation.22 | async-start | bytes 2621440 | tf_op jit(solution)/shard_map/all_gather | solution.py:73
  181.8 115.0 %reduce-scatter.22.cloned.1.call-start = ((), (), s32[]{:S(2)}) async-start(), calls=%async_computation.24 | async-start | bytes 5242880 | tf_op jit(solution)/shard_map/reduce_scatter | solution.py:85
  211.3 13.6 %collective-permute-start.2 = (bf16[1024,256]{1,0:T(8,128)(2,1)S(1)}, bf16[1024,256]{1,0:T(8,128)(2,1)}, u32[]{:S(2)}, u32[]{:S(2)}) collective-permute-start(bf16[1024,256]{1,0:T(8,128)(2,1)S(1)} %gather_fusion.8), channel_id=1, source_target_pairs={{0,3},{1,0},{2,1},{3,2},{4,7},{5,4},{6,5},{7,6},{8,11},{9,8},{10,9... | collective-permute-start | bytes 1572872 | tf_op jit(solution)/shard_map/ppermute | solution.py:21
  254.0 89.7 %reduce-scatter.20.cloned.1.call-start = ((), (), s32[]{:S(2)}) async-start(), calls=%async_computation.23 | async-start | bytes 5242880 | tf_op jit(solution)/shard_map/reduce_scatter | solution.py:77
  259.4 230.9 %reduce-scatter.24.cloned.1.call-start = ((), (), s32[]{:S(2)}) async-start(), calls=%async_computation.25 | async-start | bytes 5242880 | tf_op jit(solution)/shard_map/reduce_scatter | solution.py:85
  346.8 13.8 %collective-permute-start.3 = (bf16[1024,256]{1,0:T(8,128)(2,1)S(1)}, bf16[1024,256]{1,0:T(8,128)(2,1)}, u32[]{:S(2)}, u32[]{:S(2)}) collective-permute-start(bf16[1024,256]{1,0:T(8,128)(2,1)S(1)} %get-tuple-element.275), channel_id=1, source_target_pairs={{0,1},{1,2},{2,3},{3,0},{4,5},{5,6},{6,7},{7,4},{8,9},{9,10},{10,1... | collective-permute-start | bytes 1572872 | tf_op jit(solution)/shard_map/ppermute | solution.py:19
  346.8 14.2 %collective-permute-start.5 = (bf16[1024,256]{1,0:T(8,128)(2,1)S(1)}, bf16[1024,256]{1,0:T(8,128)(2,1)}, u32[]{:S(2)}, u32[]{:S(2)}) collective-permute-start(bf16[1024,256]{1,0:T(8,128)(2,1)S(1)} %get-tuple-element.275), channel_id=1, source_target_pairs={{0,3},{1,0},{2,1},{3,2},{4,7},{5,4},{6,5},{7,6},{8,11},{9,8},{10,9... | collective-permute-start | bytes 1572872 | tf_op jit(solution)/shard_map/ppermute | solution.py:21
  445.9 123.5 %reduce-scatter.42.cloned.1.call-start = ((), (), s32[]{:S(2)}) async-start(), calls=%async_computation.34 | async-start | bytes 147456
  446.7 173.8 %reduce-scatter.40.cloned.1.call-start = ((), (), s32[]{:S(2)}) async-start(), calls=%async_computation.33 | async-start | bytes 147456
  492.9 203.1 %reduce-scatter.38.cloned.1.call-start = ((), (), s32[]{:S(2)}) async-start(), calls=%async_computation.32 | async-start | bytes 3244032 | tf_op jit(solution)/shard_map/reduce_scatter | solution.py:291
  497.5 273.8 %reduce-scatter.36.cloned.1.call-start = ((), (), s32[]{:S(2)}) async-start(), calls=%async_computation.31 | async-start | bytes 3244032 | tf_op jit(solution)/shard_map/reduce_scatter | solution.py:290
  503.7 343.0 %reduce-scatter.34.cloned.1.call-start = ((), (), s32[]{:S(2)}) async-start(), calls=%async_computation.30 | async-start | bytes 3244032 | tf_op jit(solution)/shard_map/reduce_scatter | solution.py:289
  508.5 405.2 %reduce-scatter.32.cloned.1.call-start = ((), (), s32[]{:S(2)}) async-start(), calls=%async_computation.29 | async-start | bytes 1179648 | tf_op jit(solution)/shard_map/reduce_scatter | solution.py:288
  512.8 467.7 %reduce-scatter.30.cloned.1.call-start = ((), (), s32[]{:S(2)}) async-start(), calls=%async_computation.28 | async-start | bytes 1179648 | tf_op jit(solution)/shard_map/reduce_scatter | solution.py:287
  514.7 532.2 %reduce-scatter.28.cloned.1.call-start = ((), (), s32[]{:S(2)}) async-start(), calls=%async_computation.27 | async-start | bytes 1179648 | tf_op jit(solution)/shard_map/reduce_scatter | solution.py:286
  522.6 20.0 %all-to-all-start.3 = ((bf16[8,128,256]{2,1,0:T(8,128)(2,1)}), bf16[8,128,256]{2,1,0:T(8,128)(2,1)S(1)}, u32[]{:S(2)}, u32[]{:S(2)}) async-start(bf16[8,128,256]{2,1,0:T(8,128)(2,1)} %bitcast.209), calls=%async_computation.5 | async-start | bytes 1048576 | tf_op jit(solution)/shard_map/all_to_all | solution.py:296
  528.2 585.3 %reduce-scatter.26.cloned.1.call-start = ((), (), s32[]{:S(2)}) async-start(), calls=%async_computation.26 | async-start | bytes 1179648 | tf_op jit(solution)/shard_map/reduce_scatter | solution.py:285
  542.6 18.6 %all-to-all-start.6 = ((bf16[8,128,256]{2,1,0:T(8,128)(2,1)}), bf16[8,128,256]{2,1,0:T(8,128)(2,1)S(1)}, u32[]{:S(2)}, u32[]{:S(2)}) async-start(bf16[8,128,256]{2,1,0:T(8,128)(2,1)} %bitcast.31), calls=%async_computation.10 | async-start | bytes 1048576 | tf_op jit(solution)/shard_map/all_to_all | solution.py:298
  561.2 60.6 %all-to-all-start.5 = ((bf16[8,128,256]{2,1,0:T(8,128)(2,1)}), bf16[8,128,256]{2,1,0:T(8,128)(2,1)S(1)}, u32[]{:S(2)}, u32[]{:S(2)}) async-start(bf16[8,128,256]{2,1,0:T(8,128)(2,1)} %bitcast.29), calls=%async_computation.9 | async-start | bytes 1048576 | tf_op jit(solution)/shard_map/all_to_all | solution.py:297
  (68 other events, 1684.7 us)
Sparse Core Ops, SparseCore 0:
  65.1 22.1 all-gather.2
  127.3 43.4 reduce-scatter.17
  181.9 23.9 all-gather.4
  254.2 42.6 reduce-scatter.21
  299.2 44.4 reduce-scatter.19
  446.0 44.2 reduce-scatter.23
  493.6 62.5 reduce-scatter.41
  559.5 60.9 reduce-scatter.39
  624.6 71.2 reduce-scatter.37
  699.9 71.3 reduce-scatter.35
  775.4 71.2 reduce-scatter.33
  850.6 63.0 reduce-scatter.31
  918.0 62.4 reduce-scatter.29
  984.4 62.4 reduce-scatter.27
  1051.0 62.4 reduce-scatter.25
